TPU v7x, 32 devices: a whole 2x2x4 slice. The times are simulated.
32 devices in a mesh: ctx: 8 (over z, x), fsdp: 4 (over y, core).
Axes of the slice: x: 2, y: 2, z: 4, core: 2. Of those that a mesh axis runs over, the one named last changes fastest.
Arguments:
- layer_input: bfloat16 [2, 4, 1024, 1024], P(None, 'fsdp', 'ctx'), may hold values from -6 to 6
- segments: int32 [2, 4, 1024], P(None, 'fsdp', 'ctx'), may hold values from 0 to 15, never falling along the last dimension, each value on 1 to 512 neighbouring positions
- cotangent: bfloat16 [2, 4, 1024, 1024], P(None, 'fsdp', 'ctx'), may hold values from -6 to 6
- query_weight: bfloat16 [1024, 1024], P('fsdp'), may hold values from -0.1875 to 0.1875
- key_weight: bfloat16 [1024, 1024], P('fsdp'), may hold values from -0.1875 to 0.1875
- value_weight: bfloat16 [1024, 1024], P('fsdp'), may hold values from -0.1875 to 0.1875
- output_weight: bfloat16 [1024, 1024], P('fsdp'), may hold values from -0.75 to 0.75
- expand_weight: bfloat16 [1024, 4096], P('fsdp'), may hold values from -0.1875 to 0.1875
- contract_weight: bfloat16 [4096, 1024], P('fsdp'), may hold values from -0.09375 to 0.09375
- query_bias: bfloat16 [1024], P('fsdp'), may hold values from -3 to 3
- value_bias: bfloat16 [1024], P('fsdp'), may hold values from -3 to 3
- output_bias: bfloat16 [1024], P('fsdp'), may hold values from -3 to 3
- first_gain: bfloat16 [1024], P('fsdp'), may hold values from 0.099609375 to 1.8984375
- first_shift: bfloat16 [1024], P('fsdp'), may hold values from -3 to 3
- expand_bias: bfloat16 [4096], P('fsdp'), may hold values from -3 to 3
- contract_bias: bfloat16 [1024], P('fsdp'), may hold values from -3 to 3
- second_gain: bfloat16 [1024], P('fsdp'), may hold values from 0.099609375 to 1.8984375
- second_shift: bfloat16 [1024], P('fsdp'), may hold values from -3 to 3
Outputs:
- layer_output: bfloat16 [2, 4, 1024, 1024], P(None, 'fsdp', 'ctx')
- input_grad: float32 [2, 4, 1024, 1024], P(None, 'fsdp', 'ctx')
- query_weight_grad: float32 [1024, 1024], P('fsdp')
- key_weight_grad: float32 [1024, 1024], P('fsdp')
- value_weight_grad: float32 [1024, 1024], P('fsdp')
- output_weight_grad: float32 [1024, 1024], P('fsdp')
- expand_weight_grad: float32 [1024, 4096], P('fsdp')
- contract_weight_grad: float32 [4096, 1024], P('fsdp')
- query_bias_grad: float32 [1024], P('fsdp')
- value_bias_grad: float32 [1024], P('fsdp')
- output_bias_grad: float32 [1024], P('fsdp')
- first_gain_grad: float32 [1024], P('fsdp')
- first_shift_grad: float32 [1024], P('fsdp')
- expand_bias_grad: float32 [4096], P('fsdp')
- contract_bias_grad: float32 [1024], P('fsdp')
- second_gain_grad: float32 [1024], P('fsdp')
- second_shift_grad: float32 [1024], P('fsdp')
Inputs may be any that keep to these rules, and one draw needn't show every extreme that they name: `segments`: in each sequence the ids never fall along the positions; each document holds 1 to 512 positions, and one holds exactly 512.
All inputs are finite; a program needn't handle non-finite values.
Results may differ from a plain program's by a relative error of at most 0.025.
Values may be sent and summed in bfloat16 or wider, within the bound.
A program may use at most 192 MiB of HBM per device.

v0:
```python
import jax
import jax.numpy as jnp
from jax import lax
from jax.sharding import PartitionSpec as P

HEADS = 16
HEAD_DIM = 64


def as_sent(x):
    return jax.tree.map(lambda a: a.astype(jnp.bfloat16) if a.dtype == jnp.float32 else a, x)


def plain_dot(left_side, right_side):
    return jnp.dot(left_side, right_side, preferred_element_type=jnp.float32)


def left_dot(left_side, right_side):
    return lax.dot_general(
        left_side, right_side, (((0,), (0,)), ((), ())), preferred_element_type=jnp.float32
    )


def right_dot(left_side, right_side):
    return lax.dot_general(
        left_side, right_side, (((1,), (1,)), ((), ())), preferred_element_type=jnp.float32
    )


def norm_forward(hidden, gain_row, offset_row):
    centre = hidden - jnp.mean(hidden, axis=-1, keepdims=True)
    inverse = lax.rsqrt(jnp.mean(centre * centre, axis=-1, keepdims=True) + 1e-05)
    normed = centre * inverse
    return (normed * gain_row.astype(jnp.float32) + offset_row.astype(jnp.float32), normed, inverse)


def norm_backward(grad_out, normed, inverse, gain_row):
    scaled = grad_out * gain_row.astype(jnp.float32)
    grad_in = inverse * (
        scaled
        - jnp.mean(scaled, axis=-1, keepdims=True)
        - normed * jnp.mean(scaled * normed, axis=-1, keepdims=True)
    )
    return (grad_in, jnp.sum(grad_out * normed, axis=0), jnp.sum(grad_out, axis=0))


def gather_weights(shards):
    return (
        lax.all_gather(shards[0], "fsdp", axis=0, tiled=True),
        lax.all_gather(shards[1], "fsdp", axis=0, tiled=True),
        lax.all_gather(shards[2], "fsdp", axis=0, tiled=True),
        lax.all_gather(shards[3], "fsdp", axis=0, tiled=True),
        lax.all_gather(shards[4], "fsdp", axis=0, tiled=True),
        lax.all_gather(shards[5], "fsdp", axis=0, tiled=True),
        lax.all_gather(shards[6], "fsdp", axis=0, tiled=True),
        lax.all_gather(shards[7], "fsdp", axis=0, tiled=True),
        lax.all_gather(shards[8], "fsdp", axis=0, tiled=True),
        lax.all_gather(shards[9], "fsdp", axis=0, tiled=True),
        lax.all_gather(shards[10], "fsdp", axis=0, tiled=True),
        lax.all_gather(shards[11], "fsdp", axis=0, tiled=True),
        lax.all_gather(shards[12], "fsdp", axis=0, tiled=True),
        lax.all_gather(shards[13], "fsdp", axis=0, tiled=True),
        lax.all_gather(shards[14], "fsdp", axis=0, tiled=True),
    )


def attend_forward(query_bf, key_bf, value_bf, seg_local):
    row_count = query_bf.shape[0]
    score_scale = HEAD_DIM ** (-0.5)
    query_heads = query_bf.reshape(row_count, HEADS, HEAD_DIM)
    run_max = jnp.full((HEADS, row_count), -1e30, jnp.float32)
    key_rows = lax.all_gather(key_bf, "ctx", axis=0, tiled=True)
    value_rows = lax.all_gather(value_bf, "ctx", axis=0, tiled=True)
    key_seg = lax.all_gather(seg_local, "ctx", axis=0, tiled=True)
    piece_rows = key_rows.shape[0]
    key_heads = key_rows.reshape(piece_rows, HEADS, HEAD_DIM)
    value_heads = value_rows.reshape(piece_rows, HEADS, HEAD_DIM)
    scores = (
        jnp.einsum("rhd,khd->hrk", query_heads, key_heads, preferred_element_type=jnp.float32)
        * score_scale
    )
    same_doc = seg_local[:, None] == key_seg[None, :]
    scores = jnp.where(same_doc[None], scores, -1e30)
    new_max = jnp.maximum(run_max, jnp.max(scores, axis=-1))
    numerators = jnp.exp(scores - new_max[..., None])
    run_sum = jnp.sum(numerators, axis=-1)
    accumulated = jnp.einsum(
        "hrk,khd->hrd",
        numerators.astype(jnp.bfloat16),
        value_heads,
        preferred_element_type=jnp.float32,
    )
    run_max, run_sum, accumulated = (new_max, run_sum, accumulated)
    context = jnp.transpose(accumulated / run_sum[..., None], (1, 0, 2)).reshape(
        row_count, HEADS * HEAD_DIM
    )
    return (context, run_max + jnp.log(run_sum))


def block_grads(
    query_heads, grad_heads, query_seg, log_sum, row_delta, key_heads, value_heads, key_seg
):
    score_scale = HEAD_DIM ** (-0.5)
    scores = (
        jnp.einsum("rhd,khd->hrk", query_heads, key_heads, preferred_element_type=jnp.float32)
        * score_scale
    )
    same_doc = query_seg[:, None] == key_seg[None, :]
    scores = jnp.where(same_doc[None], scores, -1e30)
    probs_full = jnp.exp(scores - log_sum[..., None])
    grad_probs = jnp.einsum(
        "rhd,khd->hrk", grad_heads, value_heads, preferred_element_type=jnp.float32
    )
    grad_scores = (probs_full * (grad_probs - row_delta[..., None])).astype(jnp.bfloat16)
    return (probs_full, grad_scores)


def attend_backward(query_bf, key_bf, value_bf, seg_local, context, log_sum, grad_context):
    row_count = query_bf.shape[0]
    score_scale = HEAD_DIM ** (-0.5)
    key_every, value_every, seg_every = (
        lax.all_gather(key_bf, "ctx", axis=0, tiled=True),
        lax.all_gather(value_bf, "ctx", axis=0, tiled=True),
        lax.all_gather(seg_local, "ctx", axis=0, tiled=True),
    )
    length = key_every.shape[0]
    block_len = min(512, length)
    query_heads = query_bf.reshape(row_count, HEADS, HEAD_DIM)
    grad_heads = grad_context.reshape(row_count, HEADS, HEAD_DIM)
    row_delta = jnp.sum(
        (grad_context.astype(jnp.float32) * context).reshape(row_count, HEADS, HEAD_DIM), axis=-1
    ).T

    def visit_block(grad_query, block_num):
        first_row = block_num * block_len
        key_heads = lax.dynamic_slice_in_dim(key_every, first_row, block_len, 0).reshape(
            block_len, HEADS, HEAD_DIM
        )
        value_heads = lax.dynamic_slice_in_dim(value_every, first_row, block_len, 0).reshape(
            block_len, HEADS, HEAD_DIM
        )
        key_seg = lax.dynamic_slice_in_dim(seg_every, first_row, block_len, 0)
        probs_full, grad_scores = block_grads(
            query_heads, grad_heads, seg_local, log_sum, row_delta, key_heads, value_heads, key_seg
        )
        grad_query = (
            grad_query
            + jnp.einsum("hrk,khd->rhd", grad_scores, key_heads, preferred_element_type=jnp.float32)
            * score_scale
        )
        grad_keys = (
            jnp.einsum("hrk,rhd->khd", grad_scores, query_heads, preferred_element_type=jnp.float32)
            * score_scale
        )
        grad_values = jnp.einsum(
            "hrk,rhd->khd",
            probs_full.astype(jnp.bfloat16),
            grad_heads,
            preferred_element_type=jnp.float32,
        )
        stacked = jnp.stack(
            (
                grad_keys.reshape(block_len, HEADS * HEAD_DIM),
                grad_values.reshape(block_len, HEADS * HEAD_DIM),
            ),
            axis=1,
        )
        return (grad_query, stacked)

    grad_query, pieces = lax.scan(
        visit_block,
        jnp.zeros((row_count, HEADS, HEAD_DIM), jnp.float32),
        jnp.arange(length // block_len),
    )
    key_terms = pieces.reshape(length, 2, HEADS * HEAD_DIM)
    own_rows = lax.psum_scatter(
        key_terms.astype(jnp.bfloat16), "ctx", scatter_dimension=0, tiled=True
    ).astype(jnp.float32)
    grad_keyed = own_rows[:, 0].astype(jnp.bfloat16)
    grad_valued = own_rows[:, 1].astype(jnp.bfloat16)
    grad_queries = grad_query.reshape(row_count, HEADS * HEAD_DIM).astype(jnp.bfloat16)
    return (grad_queries, grad_keyed, grad_valued)


def layer_forward(inputs, seg_local, full_weights):
    (
        query_weight,
        key_weight,
        value_weight,
        output_weight,
        expand_weight,
        contract_weight,
        query_bias,
        value_bias,
        output_bias,
        first_gain,
        first_shift,
        expand_bias,
        contract_bias,
        second_gain,
        second_shift,
    ) = full_weights
    query_bf = (plain_dot(inputs, query_weight) + query_bias.astype(jnp.float32)).astype(
        jnp.bfloat16
    )
    key_bf = plain_dot(inputs, key_weight).astype(jnp.bfloat16)
    value_bf = (plain_dot(inputs, value_weight) + value_bias.astype(jnp.float32)).astype(
        jnp.bfloat16
    )
    context, log_sum = attend_forward(query_bf, key_bf, value_bf, seg_local)
    context_bf = context.astype(jnp.bfloat16)
    first_sum = (
        inputs.astype(jnp.float32)
        + plain_dot(context_bf, output_weight)
        + output_bias.astype(jnp.float32)
    )
    first_out, normed_one, inverse_one = norm_forward(first_sum, first_gain, first_shift)
    first_bf = first_out.astype(jnp.bfloat16)
    hidden = plain_dot(first_bf, expand_weight) + expand_bias.astype(jnp.float32)
    gelled_bf = jax.nn.gelu(hidden, approximate=False).astype(jnp.bfloat16)
    second_sum = (
        first_out + plain_dot(gelled_bf, contract_weight) + contract_bias.astype(jnp.float32)
    )
    result, normed_two, inverse_two = norm_forward(second_sum, second_gain, second_shift)
    kept_state = (
        query_bf,
        key_bf,
        value_bf,
        context,
        log_sum,
        context_bf,
        normed_one,
        inverse_one,
        first_bf,
        hidden,
        gelled_bf,
        normed_two,
        inverse_two,
    )
    return (result.astype(jnp.bfloat16), kept_state)


def layer_backward(inputs, seg_local, grad_out, kept_state, full_weights):
    (
        query_weight,
        key_weight,
        value_weight,
        output_weight,
        expand_weight,
        contract_weight,
        query_bias,
        value_bias,
        output_bias,
        first_gain,
        first_shift,
        expand_bias,
        contract_bias,
        second_gain,
        second_shift,
    ) = full_weights
    (
        query_bf,
        key_bf,
        value_bf,
        context,
        log_sum,
        context_bf,
        normed_one,
        inverse_one,
        first_bf,
        hidden,
        gelled_bf,
        normed_two,
        inverse_two,
    ) = kept_state
    grad_second, second_gain_grad, second_shift_grad = norm_backward(
        grad_out.astype(jnp.float32), normed_two, inverse_two, second_gain
    )
    grad_branch = grad_second.astype(jnp.bfloat16)
    contract_weight_grad = left_dot(gelled_bf, grad_branch)
    contract_bias_grad = jnp.sum(grad_branch.astype(jnp.float32), axis=0)
    grad_gelled = right_dot(grad_branch, contract_weight)
    gelu_pull = jax.vjp(lambda values: jax.nn.gelu(values, approximate=False), hidden)[1]
    grad_hidden = gelu_pull(grad_gelled)[0].astype(jnp.bfloat16)
    expand_weight_grad = left_dot(first_bf, grad_hidden)
    expand_bias_grad = jnp.sum(grad_hidden.astype(jnp.float32), axis=0)
    grad_first = grad_second + right_dot(grad_hidden, expand_weight)
    grad_attn, first_gain_grad, first_shift_grad = norm_backward(
        grad_first, normed_one, inverse_one, first_gain
    )
    grad_attn_low = grad_attn.astype(jnp.bfloat16)
    output_weight_grad = left_dot(context_bf, grad_attn_low)
    output_bias_grad = jnp.sum(grad_attn_low.astype(jnp.float32), axis=0)
    grad_context = right_dot(grad_attn_low, output_weight).astype(jnp.bfloat16)
    grad_queries, grad_keyed, grad_valued = attend_backward(
        query_bf, key_bf, value_bf, seg_local, context, log_sum, grad_context
    )
    query_weight_grad = left_dot(inputs, grad_queries)
    key_weight_grad = left_dot(inputs, grad_keyed)
    value_weight_grad = left_dot(inputs, grad_valued)
    query_bias_grad = jnp.sum(grad_queries.astype(jnp.float32), axis=0)
    value_bias_grad = jnp.sum(grad_valued.astype(jnp.float32), axis=0)
    grad_input = (
        grad_attn
        + right_dot(grad_queries, query_weight)
        + right_dot(grad_keyed, key_weight)
        + right_dot(grad_valued, value_weight)
    )
    grad_terms = (
        query_weight_grad,
        key_weight_grad,
        value_weight_grad,
        output_weight_grad,
        expand_weight_grad,
        contract_weight_grad,
        query_bias_grad,
        value_bias_grad,
        output_bias_grad,
        first_gain_grad,
        first_shift_grad,
        expand_bias_grad,
        contract_bias_grad,
        second_gain_grad,
        second_shift_grad,
    )
    return (grad_input, grad_terms)


def per_device(
    layer_input,
    segments,
    cotangent,
    query_weight,
    key_weight,
    value_weight,
    output_weight,
    expand_weight,
    contract_weight,
    query_bias,
    value_bias,
    output_bias,
    first_gain,
    first_shift,
    expand_bias,
    contract_bias,
    second_gain,
    second_shift,
):
    shards = (
        query_weight,
        key_weight,
        value_weight,
        output_weight,
        expand_weight,
        contract_weight,
        query_bias,
        value_bias,
        output_bias,
        first_gain,
        first_shift,
        expand_bias,
        contract_bias,
        second_gain,
        second_shift,
    )
    micro_count = layer_input.shape[0]
    results = []
    grad_inputs = []
    totals = None
    for micro_step in range(micro_count):
        inputs = layer_input[micro_step, 0]
        seg_local = segments[micro_step, 0].astype(jnp.bfloat16)
        front_weights = gather_weights(shards)
        result, kept_state = layer_forward(inputs, seg_local, front_weights)
        behind = gather_weights(shards)
        grad_input, grad_terms = layer_backward(
            inputs, seg_local, cotangent[micro_step, 0], kept_state, behind
        )
        results.append(result)
        grad_inputs.append(grad_input)
        if totals is None:
            totals = grad_terms
        else:
            totals = tuple(
                (left_side + right_side for left_side, right_side in zip(totals, grad_terms))
            )
    reduced = jax.tree.map(
        lambda part: part.astype(jnp.float32),
        lax.psum_scatter(as_sent(totals), "fsdp", scatter_dimension=0, tiled=True),
    )
    summed = jax.tree.map(lambda part: part.astype(jnp.float32), lax.psum(as_sent(reduced), "ctx"))
    layer_output = jnp.stack(results, axis=0)[:, None]
    input_grad = jnp.stack(grad_inputs, axis=0)[:, None]
    return (
        layer_output,
        input_grad,
        summed[0],
        summed[1],
        summed[2],
        summed[3],
        summed[4],
        summed[5],
        summed[6],
        summed[7],
        summed[8],
        summed[9],
        summed[10],
        summed[11],
        summed[12],
        summed[13],
        summed[14],
    )


def solution(mesh):
    in_specs = (
        P(None, "fsdp", "ctx", None),
        P(None, "fsdp", "ctx"),
        P(None, "fsdp", "ctx", None),
        P("fsdp", None),
        P("fsdp", None),
        P("fsdp", None),
        P("fsdp", None),
        P("fsdp", None),
        P("fsdp", None),
        P("fsdp"),
        P("fsdp"),
        P("fsdp"),
        P("fsdp"),
        P("fsdp"),
        P("fsdp"),
        P("fsdp"),
        P("fsdp"),
        P("fsdp"),
    )
    out_specs = (
        P(None, "fsdp", "ctx", None),
        P(None, "fsdp", "ctx", None),
        P("fsdp", None),
        P("fsdp", None),
        P("fsdp", None),
        P("fsdp", None),
        P("fsdp", None),
        P("fsdp", None),
        P("fsdp"),
        P("fsdp"),
        P("fsdp"),
        P("fsdp"),
        P("fsdp"),
        P("fsdp"),
        P("fsdp"),
        P("fsdp"),
        P("fsdp"),
    )
    return jax.shard_map(
        per_device, mesh=mesh, in_specs=in_specs, out_specs=out_specs, check_vma=False
    )
```

profile of v0, /device:TPU:0, one launch (start us, length us, event | category | flops | bytes accessed | tf_op | source)
XLA Modules:
  0.0 1220.2 jit_solution(14195021096110765214)
XLA Ops:
  10.1 6.0 all-gather.3
  16.1 18.8 %all-gather.27.cloned.1.call-done = bf16[1024,1024]{1,0:T(8,128)(2,1)} async-done(((bf16[256,1024]{1,0:T(8,128)(2,1)}), bf16[1024,1024]{1,0:T(8,128)(2,1)}) %all-gather.27.cloned.1.call-update) | async-done | bytes 2097168 | tf_op jit(solution)/shard_map/all_gather | solution.py:51
  34.9 2.8 fusion.68
  37.8 21.3 %all-gather.23.cloned.1.call-done = bf16[1024,1024]{1,0:T(8,128)(2,1)} async-done(((bf16[256,1024]{1,0:T(8,128)(2,1)}), bf16[1024,1024]{1,0:T(8,128)(2,1)}) %all-gather.23.cloned.1.call-update) | async-done | bytes 2097168 | tf_op jit(solution)/shard_map/all_gather | solution.py:50
  59.1 2.7 convolution_convert_fusion.3
  63.1 2.7 convolution_convert_fusion.2
  68.2 5.1 all-gather.7
  73.3 5.2 all_gather.55
  78.4 5.1 all-gather.4
  83.5 5.1 all-gather.2
  88.6 5.1 all-gather.6
  93.7 5.1 all-gather.5
  98.8 5.1 all-gather.8
  103.9 20.6 %all-gather = bf16[1,1,1024]{2,1,0:T(2,128)(2,1)S(1)} all-gather(bf16[1,1,128]{2,1,0:T(2,128)(2,1)S(1)} %get-tuple-element.466), channel_id=2, replica_groups=mesh['ctx'=8,'fsdp'=4] {'ctx'}, dimensions={2}, use_global_device_ids=true | all-gather | bytes 2304 | tf_op jit(solution)/shard_map/all_gather | solution.py:74
  124.6 16.3 %all-gather.1 = bf16[1,1,1024]{2,1,0:T(2,128)(2,1)S(1)} all-gather(bf16[1,1,128]{2,1,0:T(2,128)(2,1)S(1)} %get-tuple-element.465), channel_id=3, replica_groups=mesh['ctx'=8,'fsdp'=4] {'ctx'}, dimensions={2}, use_global_device_ids=true | all-gather | bytes 2304 | tf_op jit(solution)/shard_map/all_gather | solution.py:74
  140.9 5.4 all-gather.9
  150.3 4.0 copy.99
  154.3 31.3 %all-gather.25.cloned.1.call-done = bf16[1024,1024]{1,0:T(8,128)(2,1)} async-done(((bf16[128,1024]{1,0:T(8,128)(2,1)}), bf16[1024,1024]{1,0:T(8,128)(2,1)}) %all-gather.25.cloned.1.call-update) | async-done | bytes 2097168 | tf_op jit(solution)/shard_map/all_gather | solution.py:72
  185.6 3.9 copy.98
  189.6 3.2 fusion.28
  194.9 3.6 fusion.74
  199.6 36.4 %all-gather.39.cloned.1.call-done = bf16[1024,1024]{1,0:T(8,128)(2,1)} async-done(((bf16[128,1024]{1,0:T(8,128)(2,1)}), bf16[1024,1024]{1,0:T(8,128)(2,1)}) %all-gather.39.cloned.1.call-update) | async-done | bytes 2097168 | tf_op jit(solution)/shard_map/all_gather | solution.py:73
  236.0 3.9 copy.102
  239.9 46.6 %all-gather.37.cloned.1.call-done = bf16[1024,1024]{1,0:T(8,128)(2,1)} async-done(((bf16[128,1024]{1,0:T(8,128)(2,1)}), bf16[1024,1024]{1,0:T(8,128)(2,1)}) %all-gather.37.cloned.1.call-update) | async-done | bytes 2097168 | tf_op jit(solution)/shard_map/all_gather | solution.py:72
  286.5 3.9 copy.101
  290.4 18.7 %all-gather.31.cloned.1.call-done = bf16[1024,1024]{1,0:T(8,128)(2,1)} async-done(((bf16[256,1024]{1,0:T(8,128)(2,1)}), bf16[1024,1024]{1,0:T(8,128)(2,1)}) %all-gather.31.cloned.1.call-update) | async-done | bytes 2097168 | tf_op jit(solution)/shard_map/all_gather | solution.py:52
  311.6 3.2 fusion.29
  317.0 4.4 fusion.71
  323.0 46.0 %all-gather.33.cloned.1.call-done = bf16[1024,4096]{1,0:T(8,128)(2,1)} async-done(((bf16[256,4096]{1,0:T(8,128)(2,1)}), bf16[1024,4096]{1,0:T(8,128)(2,1)}) %all-gather.33.cloned.1.call-update) | async-done | bytes 8388624 | tf_op jit(solution)/shard_map/all_gather | solution.py:53
  369.1 6.1 convolution_add_fusion.1
  375.2 53.7 %all-gather.35.cloned.1.call-done = bf16[4096,1024]{1,0:T(8,128)(2,1)} async-done(((bf16[1024,1024]{1,0:T(8,128)(2,1)}), bf16[4096,1024]{1,0:T(8,128)(2,1)}) %all-gather.35.cloned.1.call-update) | async-done | bytes 8388624 | tf_op jit(solution)/shard_map/all_gather | solution.py:54
  428.9 9.7 fusion.170
  442.2 5.7 fusion.172
  451.1 8.1 convert_reduce_fusion.1
  459.2 3.7 multiply_reduce_fusion.1
  462.9 8.1 convert_reduce_fusion
  471.0 4.4 convert_reduce_fusion.7
  477.3 2.5 broadcast.394.clone2.1
  479.9 34.4 %while.26 = (s32[]{:T(128)}, f32[128,16,64]{0,2,1:T(8,128)}, bf16[2,512,2,1024]{3,1,0,2:T(8,128)(2,1)}, s32[2]{0:T(128)S(1)}, bf16[1024,1024]{0,1:T(8,128)(2,1)}...) while((s32[]{:T(128)}, f32[128,16,64]{0,2,1:T(8,128)}, ...), condition=%wide.region_18.19_spmd.clone, body=%wide.region_17.18_spmd.clone.sunk | while | flops 684130304 | bytes 77819448 | solution.py:170
  492.5 3.0 copy.170
  509.8 3.0 copy.170
  520.9 2.5 broadcast.394.clone2
  523.5 34.9 %while.27 = (s32[]{:T(128)}, f32[128,16,64]{0,2,1:T(8,128)}, bf16[2,512,2,1024]{3,1,0,2:T(8,128)(2,1)}, s32[2]{0:T(128)S(1)}, bf16[1024,1024]{0,1:T(8,128)(2,1)}...) while((s32[]{:T(128)}, f32[128,16,64]{0,2,1:T(8,128)}, ...), condition=%wide.region_26.27_spmd.clone, body=%wide.region_25.26_spmd.clone.sunk | while | flops 684130304 | bytes 77819448 | solution.py:170
  536.5 3.0 copy.171
  546.8 2.5 fusion.285
  553.8 3.0 copy.171
  566.6 35.8 %reduce-scatter.9.cloned.1.call-done = bf16[128,2,1024]{2,0,1:T(8,128)(2,1)} async-done(((bf16[1024,2,1024]{2,0,1:T(8,128)(2,1)}), bf16[128,2,1024]{2,0,1:T(8,128)(2,1)}) %reduce-scatter.9.cloned.1.call-update) | async-done | bytes 524304 | tf_op jit(solution)/shard_map/reduce_scatter | solution.py:176
  602.4 3.7 fusion.111
  606.1 88.5 %reduce-scatter.11.cloned.1.call-done = bf16[128,2,1024]{2,0,1:T(8,128)(2,1)} async-done(((bf16[1024,2,1024]{2,0,1:T(8,128)(2,1)}), bf16[128,2,1024]{2,0,1:T(8,128)(2,1)}) %reduce-scatter.11.cloned.1.call-update) | async-done | bytes 524304 | tf_op jit(solution)/shard_map/reduce_scatter | solution.py:176
  694.7 4.3 fusion.53
  704.2 8.2 fusion.164
  712.5 11.8 add_convert_fusion.1
  725.9 10.9 fusion.148
  736.8 12.7 %add_convert_fusion = bf16[4096,1024]{1,0:T(8,128)(2,1)} fusion(f32[4096,1024]{1,0:T(8,128)} %fusion.148, f32[128,1024]{1,0:T(8,128)S(1)} %copy-done.51, f32[128,4096]{1,0:T(8,128)S(1)} %copy-done.46), kind=kOutput, calls=%fused_computation.44 | convolution fusion | flops 1116340224 | bytes 27787264 | tf_op jit(solution)/shard_map/dot_general | solution.py:19
  749.9 12.6 %reduce-scatter.19.cloned.1.call-done = bf16[256,1024]{1,0:T(8,128)(2,1)} async-done(((bf16[1024,1024]{1,0:T(8,128)(2,1)}), bf16[256,1024]{1,0:T(8,128)(2,1)}) %reduce-scatter.19.cloned.1.call-update) | async-done | bytes 524304 | tf_op jit(solution)/shard_map/reduce_scatter | solution.py:389
  762.4 34.4 %reduce-scatter.15.cloned.1.call-done = bf16[256,1024]{0,1:T(8,128)(2,1)} async-done(((bf16[1024,1024]{0,1:T(8,128)(2,1)}), bf16[256,1024]{0,1:T(8,128)(2,1)}) %reduce-scatter.15.cloned.1.call-update) | async-done | bytes 524304 | tf_op jit(solution)/shard_map/reduce_scatter | solution.py:389
  796.8 34.6 %reduce-scatter.17.cloned.1.call-done = bf16[256,1024]{0,1:T(8,128)(2,1)} async-done(((bf16[1024,1024]{0,1:T(8,128)(2,1)}), bf16[256,1024]{0,1:T(8,128)(2,1)}) %reduce-scatter.17.cloned.1.call-update) | async-done | bytes 524304 | tf_op jit(solution)/shard_map/reduce_scatter | solution.py:389
  831.4 74.2 %reduce-scatter.21.cloned.1.call-done = bf16[256,4096]{1,0:T(8,128)(2,1)} async-done(((bf16[1024,4096]{1,0:T(8,128)(2,1)}), bf16[256,4096]{1,0:T(8,128)(2,1)}) %reduce-scatter.21.cloned.1.call-update) | async-done | bytes 2097168 | tf_op jit(solution)/shard_map/reduce_scatter | solution.py:389
  905.6 74.4 %reduce-scatter.23.cloned.1.call-done = bf16[1024,1024]{1,0:T(8,128)(2,1)} async-done(((bf16[4096,1024]{1,0:T(8,128)(2,1)}), bf16[1024,1024]{1,0:T(8,128)(2,1)}) %reduce-scatter.23.cloned.1.call-update) | async-done | bytes 2097168 | tf_op jit(solution)/shard_map/reduce_scatter | solution.py:389
  985.7 2.6 convolution_add_fusion.4
  990.1 11.3 all-reduce.11
  1002.0 23.1 %all-reduce.9 = (bf16[256]{0:T(256)(128)(2,1)S(1)}, bf16[256]{0:T(256)(128)(2,1)S(1)}, bf16[256]{0:T(256)(128)(2,1)S(1)}, bf16[256]{0:T(256)(128)(2,1)S(1)}, bf1...) all-reduce(bf16[256]{0:T(256)(128)(2,1)S(1)} %dynamic-slice.1, ...), channel_id=1, replica_groups=mesh['ctx'=8,'fsdp'=4] {'ctx'}, use_global_device_ids=true, to_apply=%region_43.44 | all-reduce | flops 3072 | bytes 12288 | tf_op jit(solution)/shard_map/psum | solution.py:391
  1030.3 2.6 convolution_add_fusion.3
  1037.3 164.2 %all-reduce.14.cloned.1.call-done = (bf16[256,1024]{0,1:T(8,128)(2,1)}, bf16[256,1024]{0,1:T(8,128)(2,1)}, bf16[256,1024]{0,1:T(8,128)(2,1)}, bf16[256,1024]{1,0...) async-done(((bf16[256,1024]{0,1:T(8,128)(2,1)}, bf16[256,1024]{0,1:T(8,128)(2,1)}, bf16[256,1024]{0,1:T(8,128)(2,1)}, bf16[256,1024]{1,0:T(8,128)(2,1)}, ...) | async-done | bytes 6291472 | tf_op jit(solution)/shard_map/psum | solution.py:391
  (424 shorter events, 129.6 us)
Async XLA Ops:
  7.2 27.7 %all-gather.27.cloned.1.call-start = ((), (), s32[]{:S(2)}) async-start(), calls=%async_computation.11 | async-start | bytes 2621440 | tf_op jit(solution)/shard_map/all_gather | solution.py:51
  7.9 51.2 %copy-start.13 = (bf16[2,1,128,1024]{3,2,1,0:T(8,128)(2,1)S(1)}, bf16[2,1,128,1024]{3,2,1,0:T(8,128)(2,1)}, u32[]{:S(2)}) copy-start(bf16[2,1,128,1024]{3,2,1,0:T(8,128)(2,1)} %param.22) | copy-start | bytes 1572868
  7.9 51.2 %all-gather.23.cloned.1.call-start = ((), (), s32[]{:S(2)}) async-start(), calls=%async_computation.9 | async-start | bytes 2621440 | tf_op jit(solution)/shard_map/all_gather | solution.py:50
  8.7 138.5 %all-gather.21.cloned.1.call-start = ((), (), s32[]{:S(2)}) async-start(), calls=%async_computation.8 | async-start | bytes 2621440 | tf_op jit(solution)/shard_map/all_gather | solution.py:49
  9.4 140.9 %all-gather.29.cloned.1.call-start = ((), (), s32[]{:S(2)}) async-start(), calls=%async_computation.12 | async-start | bytes 2359296 | tf_op jit(solution)/shard_map/all_gather | solution.py:73
  37.7 24.2 %copy-start.6 = (bf16[1024,1024]{1,0:T(8,128)(2,1)S(1)}, bf16[1024,1024]{1,0:T(8,128)(2,1)}, u32[]{:S(2)}) copy-start(bf16[1024,1024]{1,0:T(8,128)(2,1)} %all-gather.27.cloned.1.call-done) | copy-start | bytes 6291460
  37.8 147.9 %all-gather.25.cloned.1.call-start = ((), (), s32[]{:S(2)}) async-start(), calls=%async_computation.10 | async-start | bytes 2359296 | tf_op jit(solution)/shard_map/all_gather | solution.py:72
  61.9 174.1 %all-gather.39.cloned.1.call-start = ((), (), s32[]{:S(2)}) async-start(), calls=%async_computation.17 | async-start | bytes 2359296 | tf_op jit(solution)/shard_map/all_gather | solution.py:73
  63.1 223.4 %all-gather.37.cloned.1.call-start = ((), (), s32[]{:S(2)}) async-start(), calls=%async_computation.16 | async-start | bytes 2359296 | tf_op jit(solution)/shard_map/all_gather | solution.py:72
  65.9 243.3 %all-gather.31.cloned.1.call-start = ((), (), s32[]{:S(2)}) async-start(), calls=%async_computation.13 | async-start | bytes 2621440 | tf_op jit(solution)/shard_map/all_gather | solution.py:52
  66.7 6.6 copy-start.89
  66.7 11.7 copy-start.93
  66.7 16.8 %copy-start.90 = (s32[2,1,128]{2,1,0:T(1,128)S(1)}, s32[2,1,128]{2,1,0:T(1,128)}, u32[]{:S(2)}) copy-start(s32[2,1,128]{2,1,0:T(1,128)} %param.23) | copy-start | bytes 3076
  66.7 16.8 %copy-start.94 = (bf16[256]{0:T(256)(128)(2,1)S(1)}, bf16[256]{0:T(256)(128)(2,1)}, u32[]{:S(2)}) copy-start(bf16[256]{0:T(256)(128)(2,1)} %param.31) | copy-start | bytes 1540
  66.7 21.9 %copy-start.95 = (bf16[256]{0:T(256)(128)(2,1)S(1)}, bf16[256]{0:T(256)(128)(2,1)}, u32[]{:S(2)}) copy-start(bf16[256]{0:T(256)(128)(2,1)} %param.35) | copy-start | bytes 1540
  66.7 27.0 %copy-start.96 = (bf16[256]{0:T(256)(128)(2,1)S(1)}, bf16[256]{0:T(256)(128)(2,1)}, u32[]{:S(2)}) copy-start(bf16[256]{0:T(256)(128)(2,1)} %param.34) | copy-start | bytes 1540
  66.8 32.1 %copy-start.97 = (bf16[256]{0:T(256)(128)(2,1)S(1)}, bf16[256]{0:T(256)(128)(2,1)}, u32[]{:S(2)}) copy-start(bf16[256]{0:T(256)(128)(2,1)} %param.38) | copy-start | bytes 1540
  66.8 74.1 %copy-start.98 = (bf16[256]{0:T(256)(128)(2,1)S(1)}, bf16[256]{0:T(256)(128)(2,1)}, u32[]{:S(2)}) copy-start(bf16[256]{0:T(256)(128)(2,1)} %param.39) | copy-start | bytes 1540
  66.8 302.3 %all-gather.33.cloned.1.call-start = ((), (), s32[]{:S(2)}) async-start(), calls=%async_computation.14 | async-start | bytes 10485760 | tf_op jit(solution)/shard_map/all_gather | solution.py:53
  67.5 361.4 %all-gather.35.cloned.1.call-start = ((), (), s32[]{:S(2)}) async-start(), calls=%async_computation.15 | async-start | bytes 10485760 | tf_op jit(solution)/shard_map/all_gather | solution.py:54
  68.1 534.3 %reduce-scatter.9.cloned.1.call-start = ((), (), s32[]{:S(2)}) async-start(), calls=%async_computation.18 | async-start | bytes 4718592 | tf_op jit(solution)/shard_map/reduce_scatter | solution.py:176
  93.7 346.5 %copy-start.56 = (f32[4,1,256]{2,1,0:T(1,128)}, f32[4,1,256]{2,1,0:T(1,128)S(1)}, u32[]{:S(2)}) copy-start(f32[4,1,256]{2,1,0:T(1,128)S(1)} %convert_element_type.499) | copy-start | bytes 12292
  103.9 46.1 %copy-start.70 = (bf16[128]{0:T(256)(128)(2,1)}, bf16[128]{0:T(256)(128)(2,1)S(1)}, u32[]{:S(2)}) copy-start(bf16[128]{0:T(256)(128)(2,1)S(1)} %get-tuple-element.654) | copy-start | bytes 772
  103.9 46.1 %copy-start.72 = (bf16[128]{0:T(256)(128)(2,1)}, bf16[128]{0:T(256)(128)(2,1)S(1)}, u32[]{:S(2)}) copy-start(bf16[128]{0:T(256)(128)(2,1)S(1)} %get-tuple-element.702) | copy-start | bytes 772
  124.6 25.5 %copy-start.66 = (bf16[1024]{0:T(1024)(128)(2,1)}, bf16[1024]{0:T(1024)(128)(2,1)S(1)}, u32[]{:S(2)}) copy-start(bf16[1024]{0:T(1024)(128)(2,1)S(1)} %reduce.4) | copy-start | bytes 6148
  140.9 9.2 copy-start.64
  150.2 161.3 %copy-start.4 = (bf16[128,1024]{0,1:T(8,128)(2,1)}, bf16[128,1024]{0,1:T(8,128)(2,1)S(1)}, u32[]{:S(2)}) copy-start(bf16[128,1024]{0,1:T(8,128)(2,1)S(1)} %copy.100) | copy-start | bytes 786436
  198.6 110.6 %copy-start.31 = (f32[128,16,64]{0,2,1:T(8,128)}, f32[128,16,64]{0,2,1:T(8,128)S(1)}, u32[]{:S(2)}) copy-start(f32[128,16,64]{0,2,1:T(8,128)S(1)} %fusion.74) | copy-start | bytes 1572868
  290.4 21.1 %copy-start.54 = (pred[128,1024]{1,0:T(8,128)(4,1)S(1)}, pred[128,1024]{1,0:T(8,128)(4,1)}, u32[]{:S(2)}) copy-start(pred[128,1024]{1,0:T(8,128)(4,1)} %broadcast_compare_fusion.2) | copy-start | bytes 393220
  311.3 159.6 %copy-start.15 = (f32[128,1024]{1,0:T(8,128)}, f32[128,1024]{1,0:T(8,128)S(1)}, u32[]{:S(2)}) copy-start(f32[128,1024]{1,0:T(8,128)S(1)} %get-tuple-element.470) | copy-start | bytes 1572868
  311.3 159.6 %copy-start.74 = (f32[128]{0:T(128)}, f32[128]{0:T(128)S(1)}, u32[]{:S(2)}) copy-start(f32[128]{0:T(128)S(1)} %broadcast_multiply_fusion.11) | copy-start | bytes 1540
  323.0 148.0 %copy-start.76 = (f32[128]{0:T(128)}, f32[128]{0:T(128)S(1)}, u32[]{:S(2)}) copy-start(f32[128]{0:T(128)S(1)} %add_rsqrt_fusion.3) | copy-start | bytes 1540
  428.9 9.9 slice-start
  428.9 9.9 slice-start.1
  428.9 9.9 copy-start.18
  442.2 20.6 %copy-start.45 = (f32[128,4096]{1,0:T(8,128)}, f32[128,4096]{1,0:T(8,128)S(1)}, u32[]{:S(2)}) copy-start(f32[128,4096]{1,0:T(8,128)S(1)} %convolution_add_fusion) | copy-start | bytes 6291460
  442.2 5.9 copy-start.30
  451.1 8.1 copy-start.52
  451.1 19.9 %copy-start.50 = (f32[128,1024]{1,0:T(8,128)}, f32[128,1024]{1,0:T(8,128)S(1)}, u32[]{:S(2)}) copy-start(f32[128,1024]{1,0:T(8,128)S(1)} %get-tuple-element.439) | copy-start | bytes 1572868
  514.4 180.3 %reduce-scatter.11.cloned.1.call-start = ((), (), s32[]{:S(2)}) async-start(), calls=%async_computation.19 | async-start | bytes 4718592 | tf_op jit(solution)/shard_map/reduce_scatter | solution.py:176
  558.4 191.5 %reduce-scatter.13.cloned.1.call-start = ((), (), s32[]{:S(2)}) async-start(), calls=%async_computation.20 | async-start | bytes 2621440 | tf_op jit(solution)/shard_map/reduce_scatter | solution.py:389
  562.7 199.7 %reduce-scatter.19.cloned.1.call-start = ((), (), s32[]{:S(2)}) async-start(), calls=%async_computation.23 | async-start | bytes 2621440 | tf_op jit(solution)/shard_map/reduce_scatter | solution.py:389
  566.6 230.2 %reduce-scatter.15.cloned.1.call-start = ((), (), s32[]{:S(2)}) async-start(), calls=%async_computation.21 | async-start | bytes 2621440 | tf_op jit(solution)/shard_map/reduce_scatter | solution.py:389
  699.0 132.4 %reduce-scatter.17.cloned.1.call-start = ((), (), s32[]{:S(2)}) async-start(), calls=%async_computation.22 | async-start | bytes 2621440 | tf_op jit(solution)/shard_map/reduce_scatter | solution.py:389
  702.9 9.6 copy-start.20
  702.9 202.7 %reduce-scatter.21.cloned.1.call-start = ((), (), s32[]{:S(2)}) async-start(), calls=%async_computation.24 | async-start | bytes 10485760 | tf_op jit(solution)/shard_map/reduce_scatter | solution.py:389
  704.2 8.2 copy-start.36
  724.3 255.6 %reduce-scatter.23.cloned.1.call-start = ((), (), s32[]{:S(2)}) async-start(), calls=%async_computation.25 | async-start | bytes 10485760 | tf_op jit(solution)/shard_map/reduce_scatter | solution.py:389
  725.9 10.9 copy-start.46
  725.9 10.9 copy-start.51
  749.6 451.9 %all-reduce.14.cloned.1.call-start = ((), (), s32[]{:S(2)}) async-start(), calls=%async_computation.26 | async-start | bytes 12582912 | tf_op jit(solution)/shard_map/psum | solution.py:391
  979.9 5.6 copy-start.85
  979.9 5.7 copy-start.78
  980.0 5.7 copy-start.84
  980.0 5.7 copy-start.82
  980.0 5.7 copy-start.83
  980.0 5.7 copy-start.80
  980.0 5.7 copy-start.81
  980.0 5.7 copy-start.87
  980.0 5.7 copy-start.88
  980.0 5.7 copy-start.10
  990.0 42.9 %copy-start.7 = (bf16[1024,1024]{1,0:T(8,128)(2,1)S(1)}, bf16[1024,1024]{1,0:T(8,128)(2,1)}, u32[]{:S(2)}) copy-start(bf16[1024,1024]{1,0:T(8,128)(2,1)} %all-gather.27.cloned.1.call-done) | copy-start | bytes 6291460
  990.0 42.9 %copy-start.41 = (bf16[128,2,1024]{2,0,1:T(8,128)(2,1)S(1)}, bf16[128,2,1024]{2,0,1:T(8,128)(2,1)}, u32[]{:S(2)}) copy-start(bf16[128,2,1024]{2,0,1:T(8,128)(2,1)} %reduce-scatter.11.cloned.1.call-done) | copy-start | bytes 1572868
  1201.5 5.9 copy-start.58
  (63 other events, 138.7 us)
Sparse Core Ops, SparseCore 0:
  9.6 25.2 all-gather.26
  36.5 22.5 all-gather.22
  60.7 22.6 all-gather.20
  85.9 49.3 all-gather.28
  137.8 47.7 all-gather.24
  188.2 47.7 all-gather.38
  238.7 47.7 all-gather.36
  288.1 21.0 all-gather.30
  310.8 58.2 all-gather.32
  370.5 58.3 all-gather.34
  514.5 87.8 reduce-scatter.8
  606.9 87.6 reduce-scatter.10
  697.2 31.1 reduce-scatter.12
  730.9 31.4 reduce-scatter.18
  765.4 31.4 reduce-scatter.14
  799.9 31.3 reduce-scatter.16
  833.8 71.7 reduce-scatter.20
  908.2 71.6 reduce-scatter.22
  984.9 216.5 all-reduce.13
where the time goes:
time: 1230 us; the launch traced here: 1220 us
  waiting for transfers between devices  796 us (65%)
  matrix products  178 us (14%)
  blocking collectives  118 us (10%)
  local copies, waits for them, and re-layouts  74.1 us (6%)
  other arithmetic  32.8 us (3%)
  between operations  16.8 us (1%)
    reduce_scatter x6, waiting for transfers between devices, per_device(): lax.psum_scatter(as_sent(totals), 'fsdp', scatter_dimension=0, tiled=True)  230 us
    psum x1, waiting for transfers between devices, per_device(): lax.psum(as_sent(reduced), 'ctx')  164 us
    reduce_scatter x2, waiting for transfers between devices, attend_backward(): lax.psum_scatter(key_terms.astype(jnp.bfloat16), 'ctx', scatter_dimension...  124 us
    all_gather x2, waiting for transfers between devices, attend_forward(): key_rows = lax.all_gather(key_bf, 'ctx', axis=0, tiled=True)  77.9 us
    dot_general x12, matrix products, left_dot(): lax.dot_general(left_side, right_side, (((0,), (0,)), ((), ())), preferre...  60 us
    all_gather x1, waiting for transfers between devices, gather_weights(): lax.all_gather(shards[5], 'fsdp', axis=0, tiled=True)  53.7 us
    all_gather x1, waiting for transfers between devices, gather_weights(): lax.all_gather(shards[4], 'fsdp', axis=0, tiled=True)  46 us
    dot_general x12, matrix products, plain_dot(): return jnp.dot(left_side, right_side, preferred_element_type=jnp.float32)  37.6 us
  transfers between devices with their start and end apart: 19, of which 16 were waited for; matrix products, arithmetic and copies ran while one was open for 15% of the time, Pallas kernels for 0%

commit v1 on v0

--- a/solution.py
+++ b/solution.py
@@ -5,6 +5,18 @@
 
 HEADS = 16
 HEAD_DIM = 64
+
+
+def collect(x, axis, dim):
+    ways, here, step = (lax.axis_size(axis), lax.axis_index(axis), x.shape[dim])
+    line, have = (x, 1)
+    while have < ways:
+        line = jnp.concatenate(
+            [line, lax.ppermute(line, axis, [(d, (d - have) % ways) for d in range(ways)])],
+            axis=dim,
+        )
+        have = 2 * have
+    return jnp.roll(line, here * step, axis=dim)
 
 
 def as_sent(x):
@@ -51,7 +63,7 @@
         lax.all_gather(shards[2], "fsdp", axis=0, tiled=True),
         lax.all_gather(shards[3], "fsdp", axis=0, tiled=True),
         lax.all_gather(shards[4], "fsdp", axis=0, tiled=True),
-        lax.all_gather(shards[5], "fsdp", axis=0, tiled=True),
+        collect(shards[5], "fsdp", 0),
         lax.all_gather(shards[6], "fsdp", axis=0, tiled=True),
         lax.all_gather(shards[7], "fsdp", axis=0, tiled=True),
         lax.all_gather(shards[8], "fsdp", axis=0, tiled=True),

time: 1230 us -> 1180 us (0.959)
  waiting for transfers between devices: 796 us -> 638 us
  blocking collectives: 118 us -> 205 us
  other arithmetic: 32.8 us -> 53.9 us
    all_gather x1, blocking collectives: 5.08 us -> 92.5 us  [gather_weights(): lax.all_gather(shards[12], 'fsdp', axis=0, tiled=True)]
    all_gather x2, waiting for transfers between devices: 77.9 us -> 0.01 us  [attend_forward(): key_rows = lax.all_gather(key_bf, 'ctx', axis=0, tiled=True)]
    all_gather x1 -> x0, waiting for transfers between devices: 53.7 us -> none  [gather_weights(): lax.all_gather(shards[5], 'fsdp', axis=0, tiled=True)]
    all_gather x2, waiting for transfers between devices: 36.4 us -> 0.01 us  [attend_forward(): value_rows = lax.all_gather(value_bf, 'ctx', axis=0, tiled=True)]
    ppermute x0 -> x2, waiting for transfers between devices: none -> 34.2 us  [collect(): lax.ppermute(line, axis, [(d, (d - have) % ways) for d in range(ways)])]
    concatenate x0 -> x2, other arithmetic: none -> 21.1 us  [the longest x1 17 us: collect(): return jnp.roll(line, here * step, axis=dim)]
    all_gather x1, waiting for transfers between devices: 18.7 us -> 0.01 us  [gather_weights(): lax.all_gather(shards[3], 'fsdp', axis=0, tiled=True)]
  transfers between devices with their start and end apart: 19 -> 20, of which waited for: 16 -> 12; matrix products, arithmetic and copies ran while one was open for 15% -> 17% of each run, Pallas kernels for 0% -> 0%
where the time goes in v1:
time: 1180 us; the launch traced here: 1170 us
  waiting for transfers between devices  638 us (54%)
  blocking collectives  205 us (17%)
  matrix products  177 us (15%)
  local copies, waits for them, and re-layouts  72.1 us (6%)
  other arithmetic  53.9 us (5%)
  between operations  17.3 us (1%)
    reduce_scatter x6, waiting for transfers between devices, per_device(): lax.psum_scatter(as_sent(totals), 'fsdp', scatter_dimension=0, tiled=True)  230 us
    psum x1, waiting for transfers between devices, per_device(): lax.psum(as_sent(reduced), 'ctx')  164 us
    reduce_scatter x2, waiting for transfers between devices, attend_backward(): lax.psum_scatter(key_terms.astype(jnp.bfloat16), 'ctx', scatter_dimension...  125 us
    all_gather x1, blocking collectives, gather_weights(): lax.all_gather(shards[12], 'fsdp', axis=0, tiled=True)  92.5 us
    dot_general x12, matrix products, left_dot(): lax.dot_general(left_side, right_side, (((0,), (0,)), ((), ())), preferre...  60 us
    all_gather x1, waiting for transfers between devices, gather_weights(): lax.all_gather(shards[4], 'fsdp', axis=0, tiled=True)  41.1 us
    all_gather x2, blocking collectives, attend_forward(): key_seg = lax.all_gather(seg_local, 'ctx', axis=0, tiled=True)  36.6 us
    dot_general x12, matrix products, right_dot(): lax.dot_general(left_side, right_side, (((1,), (1,)), ((), ())), preferre...  36.4 us
  transfers between devices with their start and end apart: 20, of which 12 were waited for; matrix products, arithmetic and copies ran while one was open for 17% of the time, Pallas kernels for 0%

profile of v1, /device:TPU:0, one launch (start us, length us, event | category | flops | bytes accessed | tf_op | source)
XLA Modules:
  0.0 1169.8 jit_solution(15967095938438934123)
XLA Ops:
  10.1 6.0 all-gather.3
  16.1 18.8 %all-gather.26.cloned.1.call-done = bf16[1024,1024]{1,0:T(8,128)(2,1)} async-done(((bf16[256,1024]{1,0:T(8,128)(2,1)}), bf16[1024,1024]{1,0:T(8,128)(2,1)}) %all-gather.26.cloned.1.call-update) | async-done | bytes 2097168 | tf_op jit(solution)/shard_map/all_gather | solution.py:63
  34.9 2.8 fusion.73
  37.8 21.3 %all-gather.22.cloned.1.call-done = bf16[1024,1024]{1,0:T(8,128)(2,1)} async-done(((bf16[256,1024]{1,0:T(8,128)(2,1)}), bf16[1024,1024]{1,0:T(8,128)(2,1)}) %all-gather.22.cloned.1.call-update) | async-done | bytes 2097168 | tf_op jit(solution)/shard_map/all_gather | solution.py:62
  59.1 2.7 convolution_convert_fusion.3
  63.1 2.9 convolution_convert_fusion.2
  67.7 34.2 %collective-permute-done = bf16[1024,1024]{1,0:T(8,128)(2,1)} collective-permute-done((bf16[1024,1024]{1,0:T(8,128)(2,1)S(1)}, bf16[1024,1024]{1,0:T(8,128)(2,1)}, u32[]{:S(2)}, u32[]{:S(2)}) %collective-permute-start) | collective-permute-done | bytes 2097184 | tf_op jit(solution)/shard_map/ppermute | solution.py:15
  101.9 4.0 pad_maximum_fusion
  107.6 92.5 %all-gather.7 = bf16[4,1,256]{2,1,0:T(2,128)(2,1)S(1)} all-gather(bf16[1,1,256]{2,1,0:T(2,128)(2,1)S(1)} %reshape.371), channel_id=1, replica_groups=mesh['ctx'=8,'fsdp'=4] {'fsdp'}, dimensions={0}, use_global_device_ids=true | all-gather | bytes 2560 | tf_op jit(solution)/shard_map/all_gather | solution.py:73
  200.1 5.5 all_gather.53
  205.6 5.1 all-gather.4
  210.7 5.1 all-gather.2
  215.8 5.1 all-gather.6
  220.9 5.1 all-gather.5
  226.0 5.1 all-gather.8
  231.1 20.4 %all-gather = bf16[1,1,1024]{2,1,0:T(2,128)(2,1)S(1)} all-gather(bf16[1,1,128]{2,1,0:T(2,128)(2,1)S(1)} %get-tuple-element.467), channel_id=2, replica_groups=mesh['ctx'=8,'fsdp'=4] {'ctx'}, dimensions={2}, use_global_device_ids=true | all-gather | bytes 2304 | tf_op jit(solution)/shard_map/all_gather | solution.py:86
  251.5 16.2 %all-gather.1 = bf16[1,1,1024]{2,1,0:T(2,128)(2,1)S(1)} all-gather(bf16[1,1,128]{2,1,0:T(2,128)(2,1)S(1)} %get-tuple-element.466), channel_id=3, replica_groups=mesh['ctx'=8,'fsdp'=4] {'ctx'}, dimensions={2}, use_global_device_ids=true | all-gather | bytes 2304 | tf_op jit(solution)/shard_map/all_gather | solution.py:86
  267.7 5.1 all-gather.9
  276.9 17.0 %fusion.30 = bf16[4096,1024]{1,0:T(8,128)(2,1)} fusion(s32[]{:T(128)S(6)} %select_n.41, bf16[1024,1024]{1,0:T(8,128)(2,1)} %param.32, bf16[1024,1024]{1,0:T(8,128)(2,1)} %collective-permute-done, bf16[2048,1024]{1,0:T(8,128)(2,1)} %collective-permute-done.1), kind=kLoop, calls=%fused_computation.54 | loop fusion | flops 50331648 | bytes 16777220 | tf_op jit(solution)/shard_map/jit(_roll_dynamic)/concatenate | solution.py:19
  293.9 3.9 copy.99
  297.8 4.0 copy.98
  301.8 3.2 fusion.33
  307.2 3.6 fusion.79
  311.8 4.0 copy.102
  315.8 3.9 copy.101
  322.2 3.5 fusion.34
  327.8 4.0 fusion.76
  333.5 41.1 %all-gather.32.cloned.1.call-done = bf16[1024,4096]{1,0:T(8,128)(2,1)} async-done(((bf16[256,4096]{1,0:T(8,128)(2,1)}), bf16[1024,4096]{1,0:T(8,128)(2,1)}) %all-gather.32.cloned.1.call-update) | async-done | bytes 8388624 | tf_op jit(solution)/shard_map/all_gather | solution.py:65
  374.6 4.9 convolution_add_fusion.1
  379.6 9.5 fusion.175
  390.7 5.5 fusion.177
  399.4 8.1 convert_reduce_fusion.1
  407.5 3.7 multiply_reduce_fusion.1
  411.2 8.1 convert_reduce_fusion
  419.3 4.4 convert_reduce_fusion.7
  425.6 2.5 broadcast.395.clone2.1
  428.2 34.8 %while.26 = (s32[]{:T(128)}, f32[128,16,64]{0,2,1:T(8,128)}, bf16[2,512,2,1024]{3,1,0,2:T(8,128)(2,1)}, s32[2]{0:T(128)S(1)}, bf16[1024,1024]{0,1:T(8,128)(2,1)}...) while((s32[]{:T(128)}, f32[128,16,64]{0,2,1:T(8,128)}, ...), condition=%wide.region_18.20_spmd.clone, body=%wide.region_17.19_spmd.clone.sunk | while | flops 684130304 | bytes 77819448 | solution.py:182
  441.2 3.0 copy.170
  451.5 2.5 fusion.276
  458.5 3.0 copy.170
  469.6 2.5 broadcast.395.clone2
  472.1 34.7 %while.27 = (s32[]{:T(128)}, f32[128,16,64]{0,2,1:T(8,128)}, bf16[2,512,2,1024]{3,1,0,2:T(8,128)(2,1)}, s32[2]{0:T(128)S(1)}, bf16[1024,1024]{0,1:T(8,128)(2,1)}...) while((s32[]{:T(128)}, f32[128,16,64]{0,2,1:T(8,128)}, ...), condition=%wide.region_26.28_spmd.clone, body=%wide.region_25.27_spmd.clone.sunk | while | flops 684130304 | bytes 77819448 | solution.py:182
  485.0 3.0 copy.171
  495.3 2.5 fusion.290
  502.4 3.0 copy.171
  515.2 36.1 %reduce-scatter.9.cloned.1.call-done = bf16[128,2,1024]{2,0,1:T(8,128)(2,1)} async-done(((bf16[1024,2,1024]{2,0,1:T(8,128)(2,1)}), bf16[128,2,1024]{2,0,1:T(8,128)(2,1)}) %reduce-scatter.9.cloned.1.call-update) | async-done | bytes 524304 | tf_op jit(solution)/shard_map/reduce_scatter | solution.py:188
  551.3 3.7 fusion.116
  554.9 88.9 %reduce-scatter.11.cloned.1.call-done = bf16[128,2,1024]{2,0,1:T(8,128)(2,1)} async-done(((bf16[1024,2,1024]{2,0,1:T(8,128)(2,1)}), bf16[128,2,1024]{2,0,1:T(8,128)(2,1)}) %reduce-scatter.11.cloned.1.call-update) | async-done | bytes 524304 | tf_op jit(solution)/shard_map/reduce_scatter | solution.py:188
  643.8 4.3 fusion.58
  653.4 8.2 fusion.169
  661.6 11.9 %add_convert_fusion.1 = bf16[1024,4096]{1,0:T(8,128)(2,1)} fusion(f32[1024,4096]{1,0:T(8,128)} %fusion.169, bf16[128,4096]{1,0:T(8,128)(2,1)S(1)} %copy-done.37, f32[128,1024]{1,0:T(8,128)S(1)} %copy-done.20, f32[128]{0:T(128)S(1)} %add_rsqrt_fusion.1, f32[128]{0:T(128)S(1)} %broadcast_multiply_fusion.9, f32[1024]{0:T(1024)S(1)} %bitcast.391, ...), kind=kOutput, calls=%fused_computation.51 | convolution fusion | flops 1082785792 | bytes 26747904 | tf_op jit(solution)/shard_map/dot_general | solution.py:31
  675.1 10.9 fusion.153
  686.0 12.7 %add_convert_fusion = bf16[4096,1024]{1,0:T(8,128)(2,1)} fusion(f32[4096,1024]{1,0:T(8,128)} %fusion.153, f32[128,1024]{1,0:T(8,128)S(1)} %copy-done.52, f32[128,4096]{1,0:T(8,128)S(1)} %copy-done.47), kind=kOutput, calls=%fused_computation.50 | convolution fusion | flops 1116340224 | bytes 27787264 | tf_op jit(solution)/shard_map/dot_general | solution.py:31
  699.1 12.4 %reduce-scatter.19.cloned.1.call-done = bf16[256,1024]{1,0:T(8,128)(2,1)} async-done(((bf16[1024,1024]{1,0:T(8,128)(2,1)}), bf16[256,1024]{1,0:T(8,128)(2,1)}) %reduce-scatter.19.cloned.1.call-update) | async-done | bytes 524304 | tf_op jit(solution)/shard_map/reduce_scatter | solution.py:401
  711.5 34.4 %reduce-scatter.15.cloned.1.call-done = bf16[256,1024]{0,1:T(8,128)(2,1)} async-done(((bf16[1024,1024]{0,1:T(8,128)(2,1)}), bf16[256,1024]{0,1:T(8,128)(2,1)}) %reduce-scatter.15.cloned.1.call-update) | async-done | bytes 524304 | tf_op jit(solution)/shard_map/reduce_scatter | solution.py:401
  745.9 34.5 %reduce-scatter.17.cloned.1.call-done = bf16[256,1024]{0,1:T(8,128)(2,1)} async-done(((bf16[1024,1024]{0,1:T(8,128)(2,1)}), bf16[256,1024]{0,1:T(8,128)(2,1)}) %reduce-scatter.17.cloned.1.call-update) | async-done | bytes 524304 | tf_op jit(solution)/shard_map/reduce_scatter | solution.py:401
  780.5 74.2 %reduce-scatter.21.cloned.1.call-done = bf16[256,4096]{1,0:T(8,128)(2,1)} async-done(((bf16[1024,4096]{1,0:T(8,128)(2,1)}), bf16[256,4096]{1,0:T(8,128)(2,1)}) %reduce-scatter.21.cloned.1.call-update) | async-done | bytes 2097168 | tf_op jit(solution)/shard_map/reduce_scatter | solution.py:401
  854.7 74.4 %reduce-scatter.23.cloned.1.call-done = bf16[1024,1024]{1,0:T(8,128)(2,1)} async-done(((bf16[4096,1024]{1,0:T(8,128)(2,1)}), bf16[1024,1024]{1,0:T(8,128)(2,1)}) %reduce-scatter.23.cloned.1.call-update) | async-done | bytes 2097168 | tf_op jit(solution)/shard_map/reduce_scatter | solution.py:401
  934.8 2.6 convolution_add_fusion.4
  939.2 11.3 all-reduce.11
  951.1 23.2 %all-reduce.9 = (bf16[256]{0:T(256)(128)(2,1)S(1)}, bf16[256]{0:T(256)(128)(2,1)S(1)}, bf16[256]{0:T(256)(128)(2,1)S(1)}, bf16[256]{0:T(256)(128)(2,1)S(1)}, bf1...) all-reduce(bf16[256]{0:T(256)(128)(2,1)S(1)} %dynamic-slice.1, ...), channel_id=1, replica_groups=mesh['ctx'=8,'fsdp'=4] {'ctx'}, use_global_device_ids=true, to_apply=%region_43.45 | all-reduce | flops 3072 | bytes 12288 | tf_op jit(solution)/shard_map/psum | solution.py:403
  979.4 2.6 convolution_add_fusion.3
  986.5 164.3 %all-reduce.14.cloned.1.call-done = (bf16[256,1024]{0,1:T(8,128)(2,1)}, bf16[256,1024]{0,1:T(8,128)(2,1)}, bf16[256,1024]{0,1:T(8,128)(2,1)}, bf16[256,1024]{1,0...) async-done(((bf16[256,1024]{0,1:T(8,128)(2,1)}, bf16[256,1024]{0,1:T(8,128)(2,1)}, bf16[256,1024]{0,1:T(8,128)(2,1)}, bf16[256,1024]{1,0:T(8,128)(2,1)}, ...) | async-done | bytes 6291472 | tf_op jit(solution)/shard_map/psum | solution.py:403
  1157.7 2.5 convert_element_type.463
  (432 shorter events, 123.8 us)
Async XLA Ops:
  7.2 27.7 %all-gather.26.cloned.1.call-start = ((), (), s32[]{:S(2)}) async-start(), calls=%async_computation.11 | async-start | bytes 2621440 | tf_op jit(solution)/shard_map/all_gather | solution.py:63
  7.9 51.2 %copy-start.13 = (bf16[2,1,128,1024]{3,2,1,0:T(8,128)(2,1)S(1)}, bf16[2,1,128,1024]{3,2,1,0:T(8,128)(2,1)}, u32[]{:S(2)}) copy-start(bf16[2,1,128,1024]{3,2,1,0:T(8,128)(2,1)} %param.24) | copy-start | bytes 1572868
  7.9 51.2 %all-gather.22.cloned.1.call-start = ((), (), s32[]{:S(2)}) async-start(), calls=%async_computation.9 | async-start | bytes 2621440 | tf_op jit(solution)/shard_map/all_gather | solution.py:62
  8.7 265.1 %all-gather.20.cloned.1.call-start = ((), (), s32[]{:S(2)}) async-start(), calls=%async_computation.8 | async-start | bytes 2621440 | tf_op jit(solution)/shard_map/all_gather | solution.py:61
  9.4 284.4 %all-gather.28.cloned.1.call-start = ((), (), s32[]{:S(2)}) async-start(), calls=%async_computation.12 | async-start | bytes 2359296 | tf_op jit(solution)/shard_map/all_gather | solution.py:85
  37.7 24.2 %copy-start.6 = (bf16[1024,1024]{1,0:T(8,128)(2,1)S(1)}, bf16[1024,1024]{1,0:T(8,128)(2,1)}, u32[]{:S(2)}) copy-start(bf16[1024,1024]{1,0:T(8,128)(2,1)} %all-gather.26.cloned.1.call-done) | copy-start | bytes 6291460
  37.8 260.0 %all-gather.24.cloned.1.call-start = ((), (), s32[]{:S(2)}) async-start(), calls=%async_computation.10 | async-start | bytes 2359296 | tf_op jit(solution)/shard_map/all_gather | solution.py:84
  61.9 249.9 %all-gather.36.cloned.1.call-start = ((), (), s32[]{:S(2)}) async-start(), calls=%async_computation.16 | async-start | bytes 2359296 | tf_op jit(solution)/shard_map/all_gather | solution.py:85
  63.1 252.7 %all-gather.34.cloned.1.call-start = ((), (), s32[]{:S(2)}) async-start(), calls=%async_computation.15 | async-start | bytes 2359296 | tf_op jit(solution)/shard_map/all_gather | solution.py:84
  66.0 253.7 %all-gather.30.cloned.1.call-start = ((), (), s32[]{:S(2)}) async-start(), calls=%async_computation.13 | async-start | bytes 2621440 | tf_op jit(solution)/shard_map/all_gather | solution.py:64
  66.8 307.8 %all-gather.32.cloned.1.call-start = ((), (), s32[]{:S(2)}) async-start(), calls=%async_computation.14 | async-start | bytes 10485760 | tf_op jit(solution)/shard_map/all_gather | solution.py:65
  66.9 35.0 %collective-permute-start = (bf16[1024,1024]{1,0:T(8,128)(2,1)S(1)}, bf16[1024,1024]{1,0:T(8,128)(2,1)}, u32[]{:S(2)}, u32[]{:S(2)}) collective-permute-start(bf16[1024,1024]{1,0:T(8,128)(2,1)S(1)} %copy-done.27), channel_id=1, source_target_pairs={{0,3},{1,0},{2,1},{3,2},{4,7},{5,4},{6,5},{7,6},{8,11},{9,8},{10,9... | collective-permute-start | bytes 6291464 | tf_op jit(solution)/shard_map/ppermute | solution.py:15
  67.5 40.1 %copy-start.92 = (bf16[256]{0:T(256)(128)(2,1)S(1)}, bf16[256]{0:T(256)(128)(2,1)}, u32[]{:S(2)}) copy-start(bf16[256]{0:T(256)(128)(2,1)} %param.39) | copy-start | bytes 1540
  67.5 132.6 %copy-start.90 = (bf16[1024]{0:T(1024)(128)(2,1)S(1)}, bf16[1024]{0:T(1024)(128)(2,1)}, u32[]{:S(2)}) copy-start(bf16[1024]{0:T(1024)(128)(2,1)} %param.38) | copy-start | bytes 6148
  67.6 138.1 %copy-start.93 = (bf16[256]{0:T(256)(128)(2,1)S(1)}, bf16[256]{0:T(256)(128)(2,1)}, u32[]{:S(2)}) copy-start(bf16[256]{0:T(256)(128)(2,1)} %param.35) | copy-start | bytes 1540
  67.6 143.1 %copy-start.91 = (s32[2,1,128]{2,1,0:T(1,128)S(1)}, s32[2,1,128]{2,1,0:T(1,128)}, u32[]{:S(2)}) copy-start(s32[2,1,128]{2,1,0:T(1,128)} %param.25) | copy-start | bytes 3076
  67.6 143.1 %copy-start.94 = (bf16[256]{0:T(256)(128)(2,1)S(1)}, bf16[256]{0:T(256)(128)(2,1)}, u32[]{:S(2)}) copy-start(bf16[256]{0:T(256)(128)(2,1)} %param.33) | copy-start | bytes 1540
  67.6 148.2 %copy-start.95 = (bf16[256]{0:T(256)(128)(2,1)S(1)}, bf16[256]{0:T(256)(128)(2,1)}, u32[]{:S(2)}) copy-start(bf16[256]{0:T(256)(128)(2,1)} %param.37) | copy-start | bytes 1540
  67.6 153.3 %copy-start.96 = (bf16[256]{0:T(256)(128)(2,1)S(1)}, bf16[256]{0:T(256)(128)(2,1)}, u32[]{:S(2)}) copy-start(bf16[256]{0:T(256)(128)(2,1)} %param.36) | copy-start | bytes 1540
  67.6 158.4 %copy-start.97 = (bf16[256]{0:T(256)(128)(2,1)S(1)}, bf16[256]{0:T(256)(128)(2,1)}, u32[]{:S(2)}) copy-start(bf16[256]{0:T(256)(128)(2,1)} %param.40) | copy-start | bytes 1540
  67.6 200.1 %copy-start.98 = (bf16[256]{0:T(256)(128)(2,1)S(1)}, bf16[256]{0:T(256)(128)(2,1)}, u32[]{:S(2)}) copy-start(bf16[256]{0:T(256)(128)(2,1)} %param.41) | copy-start | bytes 1540
  67.6 483.6 %reduce-scatter.9.cloned.1.call-start = ((), (), s32[]{:S(2)}) async-start(), calls=%async_computation.17 | async-start | bytes 4718592 | tf_op jit(solution)/shard_map/reduce_scatter | solution.py:188
  105.9 170.9 %collective-permute-start.1 = (bf16[2048,1024]{1,0:T(8,128)(2,1)}, bf16[2048,1024]{1,0:T(8,128)(2,1)}, u32[]{:S(2)}, u32[]{:S(2)}) collective-permute-start(bf16[2048,1024]{1,0:T(8,128)(2,1)} %pad_maximum_fusion), channel_id=1, source_target_pairs={{0,2},{1,3},{2,0},{3,1},{4,6},{5,7},{6,4},{7,5},{8,10},{9,11},{10,... | collective-permute-start | bytes 12582920 | tf_op jit(solution)/shard_map/ppermute | solution.py:15
  220.9 169.8 %copy-start.57 = (f32[4,1,256]{2,1,0:T(1,128)}, f32[4,1,256]{2,1,0:T(1,128)S(1)}, u32[]{:S(2)}) copy-start(f32[4,1,256]{2,1,0:T(1,128)S(1)} %convert_element_type.499) | copy-start | bytes 12292
  231.1 45.5 %copy-start.71 = (bf16[128]{0:T(256)(128)(2,1)}, bf16[128]{0:T(256)(128)(2,1)S(1)}, u32[]{:S(2)}) copy-start(bf16[128]{0:T(256)(128)(2,1)S(1)} %get-tuple-element.655) | copy-start | bytes 772
  231.1 45.5 %copy-start.73 = (bf16[128]{0:T(256)(128)(2,1)}, bf16[128]{0:T(256)(128)(2,1)S(1)}, u32[]{:S(2)}) copy-start(bf16[128]{0:T(256)(128)(2,1)S(1)} %get-tuple-element.703) | copy-start | bytes 772
  251.5 25.1 %copy-start.67 = (bf16[1024]{0:T(1024)(128)(2,1)}, bf16[1024]{0:T(1024)(128)(2,1)S(1)}, u32[]{:S(2)}) copy-start(bf16[1024]{0:T(1024)(128)(2,1)S(1)} %reduce.4) | copy-start | bytes 6148
  267.7 8.9 copy-start.65
  276.8 45.3 %copy-start.4 = (bf16[128,1024]{0,1:T(8,128)(2,1)}, bf16[128,1024]{0,1:T(8,128)(2,1)S(1)}, u32[]{:S(2)}) copy-start(bf16[128,1024]{0,1:T(8,128)(2,1)S(1)} %copy.100) | copy-start | bytes 786436
  310.8 8.9 copy-start.32
  321.9 97.4 %copy-start.15 = (f32[128,1024]{1,0:T(8,128)}, f32[128,1024]{1,0:T(8,128)S(1)}, u32[]{:S(2)}) copy-start(f32[128,1024]{1,0:T(8,128)S(1)} %get-tuple-element.471) | copy-start | bytes 1572868
  321.9 97.3 %copy-start.75 = (f32[128]{0:T(128)}, f32[128]{0:T(128)S(1)}, u32[]{:S(2)}) copy-start(f32[128]{0:T(128)S(1)} %broadcast_multiply_fusion.11) | copy-start | bytes 1540
  333.5 85.8 %copy-start.77 = (f32[128]{0:T(128)}, f32[128]{0:T(128)S(1)}, u32[]{:S(2)}) copy-start(f32[128]{0:T(128)S(1)} %add_rsqrt_fusion.3) | copy-start | bytes 1540
  374.6 16.1 %slice-start.2 = ((s8[8388608]{0:T(1024)(128)(4,1)}), s8[4194304]{0:T(1024)(128)(4,1)S(1)}, s32[]{:S(2)}) async-start(s8[8388608]{0:T(1024)(128)(4,1)} %bitcast.365), calls=%async_computation.28 | async-start | bytes 8388608
  379.5 19.9 %copy-start.44 = (f32[128,4096]{1,0:T(8,128)}, f32[128,4096]{1,0:T(8,128)S(1)}, u32[]{:S(2)}) copy-start(f32[128,4096]{1,0:T(8,128)S(1)} %convolution_add_fusion.1) | copy-start | bytes 6291460
  379.5 9.8 slice-start
  379.5 9.8 slice-start.1
  379.5 9.8 copy-start.18
  379.5 11.1 slice-start.3
  390.7 20.5 %copy-start.46 = (f32[128,4096]{1,0:T(8,128)}, f32[128,4096]{1,0:T(8,128)S(1)}, u32[]{:S(2)}) copy-start(f32[128,4096]{1,0:T(8,128)S(1)} %convolution_add_fusion) | copy-start | bytes 6291460
  390.7 5.8 copy-start.31
  399.4 8.1 copy-start.53
  399.4 19.9 %copy-start.51 = (f32[128,1024]{1,0:T(8,128)}, f32[128,1024]{1,0:T(8,128)S(1)}, u32[]{:S(2)}) copy-start(f32[128,1024]{1,0:T(8,128)S(1)} %get-tuple-element.440) | copy-start | bytes 1572868
  463.1 180.7 %reduce-scatter.11.cloned.1.call-start = ((), (), s32[]{:S(2)}) async-start(), calls=%async_computation.18 | async-start | bytes 4718592 | tf_op jit(solution)/shard_map/reduce_scatter | solution.py:188
  506.9 192.2 %reduce-scatter.13.cloned.1.call-start = ((), (), s32[]{:S(2)}) async-start(), calls=%async_computation.19 | async-start | bytes 2621440 | tf_op jit(solution)/shard_map/reduce_scatter | solution.py:401
  511.2 200.3 %reduce-scatter.19.cloned.1.call-start = ((), (), s32[]{:S(2)}) async-start(), calls=%async_computation.22 | async-start | bytes 2621440 | tf_op jit(solution)/shard_map/reduce_scatter | solution.py:401
  515.1 230.8 %reduce-scatter.15.cloned.1.call-start = ((), (), s32[]{:S(2)}) async-start(), calls=%async_computation.20 | async-start | bytes 2621440 | tf_op jit(solution)/shard_map/reduce_scatter | solution.py:401
  648.2 132.3 %reduce-scatter.17.cloned.1.call-start = ((), (), s32[]{:S(2)}) async-start(), calls=%async_computation.21 | async-start | bytes 2621440 | tf_op jit(solution)/shard_map/reduce_scatter | solution.py:401
  652.0 9.6 copy-start.20
  652.0 202.6 %reduce-scatter.21.cloned.1.call-start = ((), (), s32[]{:S(2)}) async-start(), calls=%async_computation.23 | async-start | bytes 10485760 | tf_op jit(solution)/shard_map/reduce_scatter | solution.py:401
  653.4 8.2 copy-start.37
  673.5 255.5 %reduce-scatter.23.cloned.1.call-start = ((), (), s32[]{:S(2)}) async-start(), calls=%async_computation.24 | async-start | bytes 10485760 | tf_op jit(solution)/shard_map/reduce_scatter | solution.py:401
  675.1 10.9 copy-start.47
  675.1 10.9 copy-start.52
  698.8 452.0 %all-reduce.14.cloned.1.call-start = ((), (), s32[]{:S(2)}) async-start(), calls=%async_computation.25 | async-start | bytes 12582912 | tf_op jit(solution)/shard_map/psum | solution.py:403
  929.1 5.7 copy-start.83
  929.1 5.7 copy-start.81
  929.1 5.7 copy-start.82
  929.1 5.7 copy-start.88
  929.1 5.7 copy-start.89
  929.1 5.7 copy-start.10
  939.0 42.9 %copy-start.7 = (bf16[1024,1024]{1,0:T(8,128)(2,1)S(1)}, bf16[1024,1024]{1,0:T(8,128)(2,1)}, u32[]{:S(2)}) copy-start(bf16[1024,1024]{1,0:T(8,128)(2,1)} %all-gather.26.cloned.1.call-done) | copy-start | bytes 6291460
  939.0 42.9 %copy-start.42 = (bf16[128,2,1024]{2,0,1:T(8,128)(2,1)S(1)}, bf16[128,2,1024]{2,0,1:T(8,128)(2,1)}, u32[]{:S(2)}) copy-start(bf16[128,2,1024]{2,0,1:T(8,128)(2,1)} %reduce-scatter.11.cloned.1.call-done) | copy-start | bytes 1572868
  1150.7 5.9 copy-start.59
  (66 other events, 159.0 us)
Sparse Core Ops, SparseCore 0:
  9.6 25.2 all-gather.25
  36.5 22.5 all-gather.21
  60.7 28.2 all-gather.19
  91.5 49.2 all-gather.27
  143.3 47.7 all-gather.23
  193.7 47.7 all-gather.35
  244.2 47.8 all-gather.33
  293.7 20.9 all-gather.29
  316.3 58.2 all-gather.31
  463.2 88.0 reduce-scatter.8
  555.9 87.8 reduce-scatter.10
  646.2 31.1 reduce-scatter.12
  680.1 31.3 reduce-scatter.18
  714.5 31.4 reduce-scatter.14
  749.0 31.3 reduce-scatter.16
  782.9 71.7 reduce-scatter.20
  857.3 71.7 reduce-scatter.22
  933.9 216.7 all-reduce.13
